TPU v7x, 32 devices: a whole 2x2x4 slice. The times are simulated.
32 devices in a mesh: groups: 2 (over x), tm: 4 (over y, core), chan: 4 (over z).
Axes of the slice: x: 2, y: 2, z: 4, core: 2. Of those that a mesh axis runs over, the one named last changes fastest.
Arguments:
- records: bfloat16 [1536, 1024], P(('groups', 'tm'), 'chan'), parts along dimension 0, may hold values from -6 to 6
- cotangent: bfloat16 [1536, 1024], P(('groups', 'tm'), 'chan'), parts along dimension 0, may hold values from -6 to 6
- filter_weight: bfloat16 [4, 2, 1024, 1024], P(None, None, 'tm', 'chan'), may hold values from -0.125 to 0.125
- gate_weight: bfloat16 [4, 2, 1024, 1024], P(None, None, 'tm', 'chan'), may hold values from -0.125 to 0.125
- mix_weight: bfloat16 [4, 1024, 1024], P(None, 'chan', 'tm'), may hold values from -0.1875 to 0.1875
Outputs:
- output: bfloat16 [1536, 1024], P(('groups', 'tm'), 'chan'), parts along dimension 0
- input_grad: bfloat16 [1536, 1024], P(('groups', 'tm'), 'chan'), parts along dimension 0
There are 2 independent parts, one for each index of `groups`. A program takes and returns all parts, laid end to end along the dimension named above; an argument that names none is the same for every part. Nothing has to cross between parts.
All inputs are finite; a program needn't handle non-finite values.
Results may differ from a plain program's by a relative error of at most 0.018.
Values may be sent and summed in bfloat16 or wider, within the bound.
A program may use at most 64 MiB of HBM per device.

v0:
```python
import jax
import jax.numpy as jnp
from jax import lax
from jax.sharding import PartitionSpec as P


def shifted(shard, axis, by):
    peers = lax.axis_size(axis)
    pairs = [(i, i + by) for i in range(peers) if 0 <= i + by < peers]
    return lax.ppermute(shard, axis, pairs)


def right_product(left, panel):
    return lax.dot_general(
        left, panel, (((1,), (1,)), ((), ())), preferred_element_type=jnp.float32
    )


def local(records, cotangent, filter_weight, gate_weight, mix_weight):
    layer_count = filter_weight.shape[0]
    tm_count = lax.axis_size("tm")
    signal = records
    stored = []
    for layer_index in range(layer_count):
        span_shards = 2**layer_index
        filt_panel, gate_panel, mix_panel = (
            lax.all_gather(filter_weight[layer_index], "tm", axis=1, tiled=True),
            lax.all_gather(gate_weight[layer_index], "tm", axis=1, tiled=True),
            lax.all_gather(mix_weight[layer_index], "tm", axis=1, tiled=True),
        )
        whole_rows = lax.all_gather(signal, "chan", axis=1, tiled=True)
        if span_shards < tm_count:
            earlier = shifted(whole_rows, "tm", span_shards)
        else:
            earlier = jnp.zeros_like(whole_rows)
        pre_filter = jnp.dot(earlier, filt_panel[0], preferred_element_type=jnp.float32) + jnp.dot(
            whole_rows, filt_panel[1], preferred_element_type=jnp.float32
        )
        pre_gate = jnp.dot(earlier, gate_panel[0], preferred_element_type=jnp.float32) + jnp.dot(
            whole_rows, gate_panel[1], preferred_element_type=jnp.float32
        )
        gated = (jnp.tanh(pre_filter) * jax.nn.sigmoid(pre_gate)).astype(jnp.bfloat16)
        mix_term = jnp.dot(gated, mix_panel, preferred_element_type=jnp.float32)
        mixed = lax.psum_scatter(
            mix_term.astype(jnp.bfloat16), "chan", scatter_dimension=1, tiled=True
        ).astype(jnp.float32)
        signal = (signal.astype(jnp.float32) + mixed).astype(jnp.bfloat16)
        stored.append((pre_filter, pre_gate, filt_panel, gate_panel, mix_panel))
    grad_now = cotangent
    for layer_index in reversed(range(layer_count)):
        span_shards = 2**layer_index
        pre_filter, pre_gate, filt_panel, gate_panel, mix_panel = stored[layer_index]
        grad_whole = lax.all_gather(grad_now, "chan", axis=1, tiled=True)
        grad_z = right_product(grad_whole, mix_panel)
        tanh_value = jnp.tanh(pre_filter)
        sig_value = jax.nn.sigmoid(pre_gate)
        grad_filt = (grad_z * sig_value * (1.0 - tanh_value * tanh_value)).astype(jnp.bfloat16)
        grad_gate = (grad_z * tanh_value * sig_value * (1.0 - sig_value)).astype(jnp.bfloat16)
        near_term = right_product(grad_filt, filt_panel[1]) + right_product(
            grad_gate, gate_panel[1]
        )
        far_term = right_product(grad_filt, filt_panel[0]) + right_product(grad_gate, gate_panel[0])
        if span_shards < tm_count:
            advanced = shifted(far_term.astype(jnp.bfloat16), "tm", -span_shards).astype(
                far_term.dtype
            )
        else:
            advanced = jnp.zeros_like(far_term)
        returned = lax.psum_scatter(
            (near_term + advanced).astype(jnp.bfloat16), "chan", scatter_dimension=1, tiled=True
        ).astype(jnp.float32)
        grad_now = (grad_now.astype(jnp.float32) + returned).astype(jnp.bfloat16)
    return (signal, grad_now)


def solution(mesh):
    return jax.shard_map(
        local,
        mesh=mesh,
        in_specs=(
            P(("groups", "tm"), "chan"),
            P(("groups", "tm"), "chan"),
            P(None, None, "tm", "chan"),
            P(None, None, "tm", "chan"),
            P(None, "chan", "tm"),
        ),
        out_specs=(P(("groups", "tm"), "chan"), P(("groups", "tm"), "chan")),
        check_vma=False,
    )
```

profile of v0, /device:TPU:0, one launch (start us, length us, event | category | flops | bytes accessed | tf_op | source)
XLA Modules:
  0.0 409.4 jit_solution(5573307418238194053)
XLA Ops:
  10.7 16.4 %all_gather.60 = bf16[192,1024]{1,0:T(8,128)(2,1)S(1)} all-gather(bf16[192,256]{1,0:T(8,128)(2,1)S(1)} %copy-done.34), channel_id=1, replica_groups=mesh['groups'=2,'tm'=4,'chan'=4] {'chan'}, dimensions={1}, use_global_device_ids=true | all-gather | bytes 491520 | tf_op jit(solution)/shard_map/all_gather | solution.py:31
  29.2 7.7 %all-gather.2 = bf16[1,256,1024]{2,1,0:T(8,128)(2,1)S(1)} all-gather(bf16[1,256,256]{2,1,0:T(8,128)(2,1)S(1)} %get-tuple-element.14), channel_id=4, replica_groups=mesh['groups'=2,'tm'=4,'chan'=4] {'tm'}, dimensions={2}, use_global_device_ids=true | all-gather | bytes 655360 | tf_op jit(solution)/shard_map/all_gather | solution.py:29
  38.3 9.2 %all-gather.23.cloned.1.call-done = bf16[1,2,1024,256]{3,2,1,0:T(8,128)(2,1)} async-done(((bf16[1,2,256,256]{3,2,1,0:T(8,128)(2,1)}), bf16[1,2,1024,256]{3,2,1,0:T(8,128)(2,1)}) %all-gather.23.cloned.1.call-update) | async-done | bytes 1048592 | tf_op jit(solution)/shard_map/all_gather | solution.py:28
  54.1 7.2 %all-gather.5 = bf16[1,256,1024]{2,1,0:T(8,128)(2,1)S(1)} all-gather(bf16[1,256,256]{2,1,0:T(8,128)(2,1)S(1)} %get-tuple-element.15), channel_id=7, replica_groups=mesh['groups'=2,'tm'=4,'chan'=4] {'tm'}, dimensions={2}, use_global_device_ids=true | all-gather | bytes 655360 | tf_op jit(solution)/shard_map/all_gather | solution.py:29
  61.3 11.6 %reduce-scatter.9.cloned.1.call-done = bf16[192,256]{1,0:T(8,128)(2,1)} async-done(((bf16[192,1024]{1,0:T(8,128)(2,1)}), bf16[192,256]{1,0:T(8,128)(2,1)}) %reduce-scatter.9.cloned.1.call-update) | async-done | bytes 98320 | tf_op jit(solution)/shard_map/reduce_scatter | solution.py:44
  73.9 14.3 %all_gather.64 = bf16[192,1024]{1,0:T(8,128)(2,1)S(1)} all-gather(bf16[192,256]{1,0:T(8,128)(2,1)S(1)} %add_convert_fusion.9), channel_id=1, replica_groups=mesh['groups'=2,'tm'=4,'chan'=4] {'chan'}, dimensions={1}, use_global_device_ids=true | all-gather | bytes 491520 | tf_op jit(solution)/shard_map/all_gather | solution.py:31
  88.2 4.1 %collective-permute-start.1 = (bf16[192,1024]{1,0:T(8,128)(2,1)S(1)}, bf16[192,1024]{1,0:T(8,128)(2,1)}, u32[]{:S(2)}, u32[]{:S(2)}) collective-permute-start(bf16[192,1024]{1,0:T(8,128)(2,1)S(1)} %all_gather.64), channel_id=1, source_target_pairs={{0,8},{4,12},{1,9},{5,13},{2,10},{6,14},{3,11},{7,15},{16,24},{20,... | collective-permute-start | bytes 1179656 | tf_op jit(solution)/shard_map/ppermute | solution.py:10
  94.4 14.1 %all-gather.27.cloned.1.call-done = bf16[1,2,1024,256]{3,2,1,0:T(8,128)(2,1)} async-done(((bf16[1,2,256,256]{3,2,1,0:T(8,128)(2,1)}), bf16[1,2,1024,256]{3,2,1,0:T(8,128)(2,1)}) %all-gather.27.cloned.1.call-update) | async-done | bytes 1048592 | tf_op jit(solution)/shard_map/all_gather | solution.py:28
  116.1 10.4 %all-gather.11 = bf16[1,256,1024]{2,1,0:T(8,128)(2,1)S(1)} all-gather(bf16[1,256,256]{2,1,0:T(8,128)(2,1)S(1)} %copy-done.33), channel_id=13, replica_groups=mesh['groups'=2,'tm'=4,'chan'=4] {'tm'}, dimensions={2}, use_global_device_ids=true | all-gather | bytes 655360 | tf_op jit(solution)/shard_map/all_gather | solution.py:29
  126.5 7.3 %all-gather.8 = bf16[1,256,1024]{2,1,0:T(8,128)(2,1)S(1)} all-gather(bf16[1,256,256]{2,1,0:T(8,128)(2,1)S(1)} %copy-done.32), channel_id=10, replica_groups=mesh['groups'=2,'tm'=4,'chan'=4] {'tm'}, dimensions={2}, use_global_device_ids=true | all-gather | bytes 655360 | tf_op jit(solution)/shard_map/all_gather | solution.py:29
  135.8 12.0 %all-gather.31.cloned.1.call-done = bf16[1,2,1024,256]{3,2,1,0:T(8,128)(2,1)} async-done(((bf16[1,2,256,256]{3,2,1,0:T(8,128)(2,1)}), bf16[1,2,1024,256]{3,2,1,0:T(8,128)(2,1)}) %all-gather.31.cloned.1.call-update) | async-done | bytes 1048592 | tf_op jit(solution)/shard_map/all_gather | solution.py:28
  149.8 21.1 %reduce-scatter.11.cloned.1.call-done = bf16[192,256]{1,0:T(8,128)(2,1)} async-done(((bf16[192,1024]{1,0:T(8,128)(2,1)}), bf16[192,256]{1,0:T(8,128)(2,1)}) %reduce-scatter.11.cloned.1.call-update) | async-done | bytes 98320 | tf_op jit(solution)/shard_map/reduce_scatter | solution.py:44
  171.9 14.3 %all_gather.69 = bf16[192,1024]{1,0:T(8,128)(2,1)S(1)} all-gather(bf16[192,256]{1,0:T(8,128)(2,1)S(1)} %add_convert_fusion.8), channel_id=1, replica_groups=mesh['groups'=2,'tm'=4,'chan'=4] {'chan'}, dimensions={1}, use_global_device_ids=true | all-gather | bytes 491520 | tf_op jit(solution)/shard_map/all_gather | solution.py:31
  189.9 14.8 %all_gather.76 = bf16[192,1024]{1,0:T(8,128)(2,1)S(1)} all-gather(bf16[192,256]{1,0:T(8,128)(2,1)S(1)} %copy-done.35), channel_id=1, replica_groups=mesh['groups'=2,'tm'=4,'chan'=4] {'chan'}, dimensions={1}, use_global_device_ids=true | all-gather | bytes 491520 | tf_op jit(solution)/shard_map/all_gather | solution.py:53
  209.8 18.9 %reduce-scatter.13.cloned.1.call-done = bf16[192,256]{1,0:T(8,128)(2,1)} async-done(((bf16[192,1024]{1,0:T(8,128)(2,1)}), bf16[192,256]{1,0:T(8,128)(2,1)}) %reduce-scatter.13.cloned.1.call-update) | async-done | bytes 98320 | tf_op jit(solution)/shard_map/reduce_scatter | solution.py:44
  230.3 14.3 %all_gather.73 = bf16[192,1024]{1,0:T(8,128)(2,1)S(1)} all-gather(bf16[192,256]{1,0:T(8,128)(2,1)S(1)} %add_convert_fusion.7), channel_id=1, replica_groups=mesh['groups'=2,'tm'=4,'chan'=4] {'chan'}, dimensions={1}, use_global_device_ids=true | all-gather | bytes 491520 | tf_op jit(solution)/shard_map/all_gather | solution.py:31
  249.2 19.7 %reduce-scatter.17.cloned.1.call-done = bf16[192,256]{1,0:T(8,128)(2,1)} async-done(((bf16[192,1024]{1,0:T(8,128)(2,1)}), bf16[192,256]{1,0:T(8,128)(2,1)}) %reduce-scatter.17.cloned.1.call-update) | async-done | bytes 98320 | tf_op jit(solution)/shard_map/reduce_scatter | solution.py:69
  270.7 14.3 %all_gather.77 = bf16[192,1024]{1,0:T(8,128)(2,1)S(1)} all-gather(bf16[192,256]{1,0:T(8,128)(2,1)S(1)} %add_convert_fusion.5), channel_id=1, replica_groups=mesh['groups'=2,'tm'=4,'chan'=4] {'chan'}, dimensions={1}, use_global_device_ids=true | all-gather | bytes 491520 | tf_op jit(solution)/shard_map/all_gather | solution.py:53
  288.2 19.6 %reduce-scatter.19.cloned.1.call-done = bf16[192,256]{1,0:T(8,128)(2,1)} async-done(((bf16[192,1024]{1,0:T(8,128)(2,1)}), bf16[192,256]{1,0:T(8,128)(2,1)}) %reduce-scatter.19.cloned.1.call-update) | async-done | bytes 98320 | tf_op jit(solution)/shard_map/reduce_scatter | solution.py:69
  308.8 14.4 %all_gather.78 = bf16[192,1024]{1,0:T(8,128)(2,1)S(1)} all-gather(bf16[192,256]{1,0:T(8,128)(2,1)S(1)} %add_convert_fusion.4), channel_id=1, replica_groups=mesh['groups'=2,'tm'=4,'chan'=4] {'chan'}, dimensions={1}, use_global_device_ids=true | all-gather | bytes 491520 | tf_op jit(solution)/shard_map/all_gather | solution.py:53
  326.8 8.0 %collective-permute-done.2 = bf16[192,1024]{1,0:T(8,128)(2,1)S(1)} collective-permute-done((bf16[192,1024]{1,0:T(8,128)(2,1)S(1)}, bf16[192,1024]{1,0:T(8,128)(2,1)S(1)}, u32[]{:S(2)}, u32[]{:S(2)}) %collective-permute-start.2) | collective-permute-done | bytes 393248 | tf_op jit(solution)/shard_map/ppermute | solution.py:10
  337.9 16.8 %reduce-scatter.21.cloned.1.call-done = bf16[192,256]{1,0:T(8,128)(2,1)} async-done(((bf16[192,1024]{1,0:T(8,128)(2,1)}), bf16[192,256]{1,0:T(8,128)(2,1)}) %reduce-scatter.21.cloned.1.call-update) | async-done | bytes 98320 | tf_op jit(solution)/shard_map/reduce_scatter | solution.py:69
  355.7 16.2 %all_gather.79 = bf16[192,1024]{1,0:T(8,128)(2,1)S(1)} all-gather(bf16[192,256]{1,0:T(8,128)(2,1)S(1)} %add_convert_fusion.3), channel_id=1, replica_groups=mesh['groups'=2,'tm'=4,'chan'=4] {'chan'}, dimensions={1}, use_global_device_ids=true | all-gather | bytes 491520 | tf_op jit(solution)/shard_map/all_gather | solution.py:53
  381.0 20.3 %reduce-scatter.23.cloned.1.call-done = bf16[192,256]{1,0:T(8,128)(2,1)} async-done(((bf16[192,1024]{1,0:T(8,128)(2,1)}), bf16[192,256]{1,0:T(8,128)(2,1)}) %reduce-scatter.23.cloned.1.call-update) | async-done | bytes 98320 | tf_op jit(solution)/shard_map/reduce_scatter | solution.py:69
  (173 shorter events, 68.0 us)
Async XLA Ops:
  7.2 29.7 %all-gather.21.cloned.1.call-start = ((), (), s32[]{:S(2)}) async-start(), calls=%async_computation.16 | async-start | bytes 1310720 | tf_op jit(solution)/shard_map/all_gather | solution.py:27
  9.6 37.9 %all-gather.23.cloned.1.call-start = ((), (), s32[]{:S(2)}) async-start(), calls=%async_computation.17 | async-start | bytes 1310720 | tf_op jit(solution)/shard_map/all_gather | solution.py:28
  10.6 17.8 %copy-start.31 = (bf16[4,256,256]{2,1,0:T(8,128)(2,1)S(1)}, bf16[4,256,256]{2,1,0:T(8,128)(2,1)}, u32[]{:S(2)}) copy-start(bf16[4,256,256]{2,1,0:T(8,128)(2,1)} %param.9) | copy-start | bytes 1572868
  10.7 62.3 %reduce-scatter.9.cloned.1.call-start = ((), (), s32[]{:S(2)}) async-start(), calls=%async_computation.8 | async-start | bytes 491520 | tf_op jit(solution)/shard_map/reduce_scatter | solution.py:44
  27.1 21.7 %collective-permute-start = (bf16[192,1024]{1,0:T(8,128)(2,1)S(1)}, bf16[192,1024]{1,0:T(8,128)(2,1)S(1)}, u32[]{:S(2)}, u32[]{:S(2)}) collective-permute-start(bf16[192,1024]{1,0:T(8,128)(2,1)S(1)} %all_gather.60), channel_id=1, source_target_pairs={{0,4},{4,8},{8,12},{1,5},{5,9},{9,13},{2,6},{6,10},{10,14},{3,7},{... | collective-permute-start | bytes 1179656 | tf_op jit(solution)/shard_map/ppermute | solution.py:10
  51.6 40.7 %all-gather.25.cloned.1.call-start = ((), (), s32[]{:S(2)}) async-start(), calls=%async_computation.18 | async-start | bytes 1310720 | tf_op jit(solution)/shard_map/all_gather | solution.py:27
  52.2 56.3 %all-gather.27.cloned.1.call-start = ((), (), s32[]{:S(2)}) async-start(), calls=%async_computation.19 | async-start | bytes 1310720 | tf_op jit(solution)/shard_map/all_gather | solution.py:28
  52.8 81.0 %all-gather.29.cloned.1.call-start = ((), (), s32[]{:S(2)}) async-start(), calls=%async_computation.20 | async-start | bytes 1310720 | tf_op jit(solution)/shard_map/all_gather | solution.py:27
  53.3 94.4 %all-gather.31.cloned.1.call-start = ((), (), s32[]{:S(2)}) async-start(), calls=%async_computation.21 | async-start | bytes 1310720 | tf_op jit(solution)/shard_map/all_gather | solution.py:28
  54.1 116.8 %reduce-scatter.11.cloned.1.call-start = ((), (), s32[]{:S(2)}) async-start(), calls=%async_computation.9 | async-start | bytes 491520 | tf_op jit(solution)/shard_map/reduce_scatter | solution.py:44
  88.2 21.7 %collective-permute-start.1 = (bf16[192,1024]{1,0:T(8,128)(2,1)S(1)}, bf16[192,1024]{1,0:T(8,128)(2,1)}, u32[]{:S(2)}, u32[]{:S(2)}) collective-permute-start(bf16[192,1024]{1,0:T(8,128)(2,1)S(1)} %all_gather.64), channel_id=1, source_target_pairs={{0,8},{4,12},{1,9},{5,13},{2,10},{6,14},{3,11},{7,15},{16,24},{20,... | collective-permute-start | bytes 1179656 | tf_op jit(solution)/shard_map/ppermute | solution.py:10
  114.4 91.3 %all-gather.33.cloned.1.call-start = ((), (), s32[]{:S(2)}) async-start(), calls=%async_computation.22 | async-start | bytes 1310720 | tf_op jit(solution)/shard_map/all_gather | solution.py:27
  115.2 92.6 %all-gather.35.cloned.1.call-start = ((), (), s32[]{:S(2)}) async-start(), calls=%async_computation.23 | async-start | bytes 1310720 | tf_op jit(solution)/shard_map/all_gather | solution.py:28
  115.8 112.9 %reduce-scatter.13.cloned.1.call-start = ((), (), s32[]{:S(2)}) async-start(), calls=%async_computation.10 | async-start | bytes 491520 | tf_op jit(solution)/shard_map/reduce_scatter | solution.py:44
  135.8 35.1 %copy-start.22 = (bf16[192,256]{1,0:T(8,128)(2,1)S(1)}, bf16[192,256]{1,0:T(8,128)(2,1)}, u32[]{:S(2)}) copy-start(bf16[192,256]{1,0:T(8,128)(2,1)} %copy-done.21) | copy-start | bytes 294916
  189.0 79.9 %reduce-scatter.17.cloned.1.call-start = ((), (), s32[]{:S(2)}) async-start(), calls=%async_computation.12 | async-start | bytes 491520 | tf_op jit(solution)/shard_map/reduce_scatter | solution.py:69
  207.7 20.9 %copy-start.24 = (bf16[192,256]{1,0:T(8,128)(2,1)S(1)}, bf16[192,256]{1,0:T(8,128)(2,1)}, u32[]{:S(2)}) copy-start(bf16[192,256]{1,0:T(8,128)(2,1)} %copy-done.23) | copy-start | bytes 294916
  249.2 58.7 %reduce-scatter.19.cloned.1.call-start = ((), (), s32[]{:S(2)}) async-start(), calls=%async_computation.13 | async-start | bytes 491520 | tf_op jit(solution)/shard_map/reduce_scatter | solution.py:69
  288.1 19.7 %copy-start.26 = (bf16[192,256]{1,0:T(8,128)(2,1)S(1)}, bf16[192,256]{1,0:T(8,128)(2,1)}, u32[]{:S(2)}) copy-start(bf16[192,256]{1,0:T(8,128)(2,1)} %copy-done.25) | copy-start | bytes 294916
  288.2 66.6 %reduce-scatter.21.cloned.1.call-start = ((), (), s32[]{:S(2)}) async-start(), calls=%async_computation.14 | async-start | bytes 491520 | tf_op jit(solution)/shard_map/reduce_scatter | solution.py:69
  325.1 9.7 %collective-permute-start.2 = (bf16[192,1024]{1,0:T(8,128)(2,1)S(1)}, bf16[192,1024]{1,0:T(8,128)(2,1)S(1)}, u32[]{:S(2)}, u32[]{:S(2)}) collective-permute-start(bf16[192,1024]{1,0:T(8,128)(2,1)S(1)} %fusion.2), channel_id=1, source_target_pairs={{8,0},{12,4},{9,1},{13,5},{10,2},{14,6},{11,3},{15,7},{24,16},{28,... | collective-permute-start | bytes 1179656 | tf_op jit(solution)/shard_map/ppermute | solution.py:10
  335.9 42.7 %reduce-scatter.15.cloned.1.call-start = ((), (), s32[]{:S(2)}) async-start(), calls=%async_computation.11 | async-start | bytes 491520 | tf_op jit(solution)/shard_map/reduce_scatter | solution.py:44
  337.9 63.5 %reduce-scatter.23.cloned.1.call-start = ((), (), s32[]{:S(2)}) async-start(), calls=%async_computation.15 | async-start | bytes 491520 | tf_op jit(solution)/shard_map/reduce_scatter | solution.py:69
  373.8 3.6 collective-permute-start.3
  (37 other events, 224.7 us)
Sparse Core Ops, SparseCore 0:
  9.7 19.4 all-gather.20
  30.7 16.6 all-gather.22
  51.7 21.1 reduce-scatter.8
  74.3 14.9 all-gather.24
  90.8 17.6 all-gather.26
  109.9 19.4 all-gather.28
  131.0 16.6 all-gather.30
  150.0 20.7 reduce-scatter.10
  172.4 14.9 all-gather.32
  188.8 16.6 all-gather.34
  207.8 20.7 reduce-scatter.12
  249.3 19.6 reduce-scatter.16
  288.3 19.5 reduce-scatter.18
  336.0 18.6 reduce-scatter.20
  356.9 19.8 reduce-scatter.14
  378.9 22.3 reduce-scatter.22
where the time goes:
time: 411 us; the launch traced here: 409 us
  waiting for transfers between devices  177 us (43%)
  blocking collectives  151 us (37%)
  matrix products  34.2 us (8%)
  local copies, waits for them, and re-layouts  14.6 us (4%)
  between operations  14.4 us (4%)
  other arithmetic  8.99 us (2%)
  starting transfers between devices  8.64 us (2%)
    reduce_scatter x4, waiting for transfers between devices, local(): lax.psum_scatter((near_term + advanced).astype(jnp.bfloat16), 'chan', sca...  76.5 us
    all_gather x4, blocking collectives, local(): grad_whole = lax.all_gather(grad_now, 'chan', axis=1, tiled=True)  59.7 us
    all_gather x4, blocking collectives, local(): whole_rows = lax.all_gather(signal, 'chan', axis=1, tiled=True)  59.3 us
    reduce_scatter x4, waiting for transfers between devices, local(): lax.psum_scatter(mix_term.astype(jnp.bfloat16), 'chan', scatter_dimension...  51.7 us
    all_gather x4, waiting for transfers between devices, local(): lax.all_gather(gate_weight[layer_index], 'tm', axis=1, tiled=True)  35.2 us
    all_gather x4, blocking collectives, local(): lax.all_gather(mix_weight[layer_index], 'tm', axis=1, tiled=True)  32.4 us
    unnamed x82, local copies, waits for them, and re-layouts  10.6 us
    ppermute x4, waiting for transfers between devices, shifted(): return lax.ppermute(shard, axis, pairs)  10 us
  transfers between devices with their start and end apart: 20, of which 12 were waited for; matrix products, arithmetic and copies ran while one was open for 8% of the time, Pallas kernels for 0%

commit v1 on v0

--- a/solution.py
+++ b/solution.py
@@ -28,7 +28,14 @@
             lax.all_gather(gate_weight[layer_index], "tm", axis=1, tiled=True),
             lax.all_gather(mix_weight[layer_index], "tm", axis=1, tiled=True),
         )
-        whole_rows = lax.all_gather(signal, "chan", axis=1, tiled=True)
+        ring = [signal]
+        for hop in range(3):
+            ring.append(lax.ppermute(ring[-1], "chan", [(dev, (dev + 1) % 4) for dev in range(4)]))
+        whole_rows = jnp.roll(
+            jnp.concatenate(ring[::-1], axis=1),
+            (lax.axis_index("chan") + 1) * ring[0].shape[1],
+            axis=1,
+        )
         if span_shards < tm_count:
             earlier = shifted(whole_rows, "tm", span_shards)
         else:

time: 411 us -> 410 us (level)
  blocking collectives: 151 us -> 91.2 us
  waiting for transfers between devices: 177 us -> 227 us
  starting transfers between devices: 8.64 us -> 17.2 us
    all_gather x4 -> x0, blocking collectives: 59.3 us -> none  [local(): whole_rows = lax.all_gather(signal, 'chan', axis=1, tiled=True)]
    ppermute x0 -> x12, waiting for transfers between devices: none -> 27.7 us  [local(): lax.ppermute(ring[-1], 'chan', [(dev, (dev + 1) % 4) for dev in range(4)])]
    all_gather x4, waiting for transfers between devices: 35.2 us -> 49.7 us  [local(): lax.all_gather(gate_weight[layer_index], 'tm', axis=1, tiled=True)]
    all_gather x4, waiting for transfers between devices: 0.01 us -> 12.2 us  [local(): lax.all_gather(filter_weight[layer_index], 'tm', axis=1, tiled=True)]
    ppermute x0 -> x12, starting transfers between devices: none -> 8.24 us  [local(): lax.ppermute(ring[-1], 'chan', [(dev, (dev + 1) % 4) for dev in range(4)])]
    reduce_scatter x4, waiting for transfers between devices: 51.7 us -> 44.9 us  [local(): lax.psum_scatter(mix_term.astype(jnp.bfloat16), 'chan', scatter_dimension...]
    all_gather x4, blocking collectives: 32.4 us -> 27.8 us  [local(): lax.all_gather(mix_weight[layer_index], 'tm', axis=1, tiled=True)]
  transfers between devices with their start and end apart: 20 -> 32, of which waited for: 12 -> 20; matrix products, arithmetic and copies ran while one was open for 8% -> 6% of each run, Pallas kernels for 0% -> 0%
where the time goes in v1:
time: 410 us; the launch traced here: 408 us
  waiting for transfers between devices  227 us (55%)
  blocking collectives  91.2 us (22%)
  matrix products  30.9 us (8%)
  starting transfers between devices  17.2 us (4%)
  local copies, waits for them, and re-layouts  15.1 us (4%)
  between operations  14.5 us (4%)
  other arithmetic  11.9 us (3%)
    reduce_scatter x4, waiting for transfers between devices, local(): lax.psum_scatter((near_term + advanced).astype(jnp.bfloat16), 'chan', sca...  78.2 us
    all_gather x4, blocking collectives, local(): grad_whole = lax.all_gather(grad_now, 'chan', axis=1, tiled=True)  63.4 us
    all_gather x4, waiting for transfers between devices, local(): lax.all_gather(gate_weight[layer_index], 'tm', axis=1, tiled=True)  49.7 us
    reduce_scatter x4, waiting for transfers between devices, local(): lax.psum_scatter(mix_term.astype(jnp.bfloat16), 'chan', scatter_dimension...  44.9 us
    all_gather x4, blocking collectives, local(): lax.all_gather(mix_weight[layer_index], 'tm', axis=1, tiled=True)  27.8 us
    ppermute x12, waiting for transfers between devices, local(): lax.ppermute(ring[-1], 'chan', [(dev, (dev + 1) % 4) for dev in range(4)])  27.7 us
    all_gather x4, waiting for transfers between devices, local(): lax.all_gather(filter_weight[layer_index], 'tm', axis=1, tiled=True)  12.2 us
    unnamed x82, local copies, waits for them, and re-layouts  11 us
  transfers between devices with their start and end apart: 32, of which 20 were waited for; matrix products, arithmetic and copies ran while one was open for 6% of the time, Pallas kernels for 0%

profile of v1, /device:TPU:0, one launch (start us, length us, event | category | flops | bytes accessed | tf_op | source)
XLA Modules:
  0.0 408.3 jit_solution(4011157352912723473)
XLA Ops:
  20.1 5.7 %collective-permute-done.1 = bf16[192,256]{1,0:T(8,128)(2,1)S(1)} collective-permute-done((bf16[192,256]{1,0:T(8,128)(2,1)S(1)}, bf16[192,256]{1,0:T(8,128)(2,1)S(1)}, u32[]{:S(2)}, u32[]{:S(2)}) %collective-permute-start.1) | collective-permute-done | bytes 98336 | tf_op jit(solution)/shard_map/ppermute | solution.py:33
  25.8 7.2 %all-gather.2 = bf16[1,256,1024]{2,1,0:T(8,128)(2,1)S(1)} all-gather(bf16[1,256,256]{2,1,0:T(8,128)(2,1)S(1)} %get-tuple-element.15), channel_id=4, replica_groups=mesh['groups'=2,'tm'=4,'chan'=4] {'tm'}, dimensions={2}, use_global_device_ids=true | all-gather | bytes 655360 | tf_op jit(solution)/shard_map/all_gather | solution.py:29
  37.3 10.1 %all-gather.23.cloned.1.call-done = bf16[1,2,1024,256]{3,2,1,0:T(8,128)(2,1)} async-done(((bf16[1,2,256,256]{3,2,1,0:T(8,128)(2,1)}), bf16[1,2,1024,256]{3,2,1,0:T(8,128)(2,1)}) %all-gather.23.cloned.1.call-update) | async-done | bytes 1048592 | tf_op jit(solution)/shard_map/all_gather | solution.py:28
  52.8 22.7 %reduce-scatter.9.cloned.1.call-done = bf16[192,256]{1,0:T(8,128)(2,1)} async-done(((bf16[192,1024]{1,0:T(8,128)(2,1)}), bf16[192,256]{1,0:T(8,128)(2,1)}) %reduce-scatter.9.cloned.1.call-update) | async-done | bytes 98320 | tf_op jit(solution)/shard_map/reduce_scatter | solution.py:51
  76.4 6.4 %collective-permute-done.4 = bf16[192,256]{1,0:T(8,128)(2,1)S(1)} collective-permute-done((bf16[192,256]{1,0:T(8,128)(2,1)S(1)}, bf16[192,256]{1,0:T(8,128)(2,1)S(1)}, u32[]{:S(2)}, u32[]{:S(2)}) %collective-permute-start.4) | collective-permute-done | bytes 98336 | tf_op jit(solution)/shard_map/ppermute | solution.py:33
  82.8 6.7 %collective-permute-done.5 = bf16[192,256]{1,0:T(8,128)(2,1)S(1)} collective-permute-done((bf16[192,256]{1,0:T(8,128)(2,1)S(1)}, bf16[192,256]{1,0:T(8,128)(2,1)S(1)}, u32[]{:S(2)}, u32[]{:S(2)}) %collective-permute-start.5) | collective-permute-done | bytes 98336 | tf_op jit(solution)/shard_map/ppermute | solution.py:33
  89.5 7.1 %all-gather.5 = bf16[1,256,1024]{2,1,0:T(8,128)(2,1)S(1)} all-gather(bf16[1,256,256]{2,1,0:T(8,128)(2,1)S(1)} %get-tuple-element.16), channel_id=7, replica_groups=mesh['groups'=2,'tm'=4,'chan'=4] {'tm'}, dimensions={2}, use_global_device_ids=true | all-gather | bytes 655360 | tf_op jit(solution)/shard_map/all_gather | solution.py:29
  102.7 9.4 %all-gather.27.cloned.1.call-done = bf16[1,2,1024,256]{3,2,1,0:T(8,128)(2,1)} async-done(((bf16[1,2,256,256]{3,2,1,0:T(8,128)(2,1)}), bf16[1,2,1024,256]{3,2,1,0:T(8,128)(2,1)}) %all-gather.27.cloned.1.call-update) | async-done | bytes 1048592 | tf_op jit(solution)/shard_map/all_gather | solution.py:28
  120.4 22.2 %reduce-scatter.11.cloned.1.call-done = bf16[192,256]{1,0:T(8,128)(2,1)} async-done(((bf16[192,1024]{1,0:T(8,128)(2,1)}), bf16[192,256]{1,0:T(8,128)(2,1)}) %reduce-scatter.11.cloned.1.call-update) | async-done | bytes 98320 | tf_op jit(solution)/shard_map/reduce_scatter | solution.py:51
  143.6 7.0 %all-gather.8 = bf16[1,256,1024]{2,1,0:T(8,128)(2,1)S(1)} all-gather(bf16[1,256,256]{2,1,0:T(8,128)(2,1)S(1)} %copy-done.34), channel_id=10, replica_groups=mesh['groups'=2,'tm'=4,'chan'=4] {'tm'}, dimensions={2}, use_global_device_ids=true | all-gather | bytes 655360 | tf_op jit(solution)/shard_map/all_gather | solution.py:29
  151.8 7.2 %all-gather.29.cloned.1.call-done = bf16[1,2,1024,256]{3,2,1,0:T(8,128)(2,1)} async-done(((bf16[1,2,256,256]{3,2,1,0:T(8,128)(2,1)}), bf16[1,2,1024,256]{3,2,1,0:T(8,128)(2,1)}) %all-gather.29.cloned.1.call-update) | async-done | bytes 1048592 | tf_op jit(solution)/shard_map/all_gather | solution.py:27
  161.9 15.4 %all-gather.31.cloned.1.call-done = bf16[1,2,1024,256]{3,2,1,0:T(8,128)(2,1)} async-done(((bf16[1,2,256,256]{3,2,1,0:T(8,128)(2,1)}), bf16[1,2,1024,256]{3,2,1,0:T(8,128)(2,1)}) %all-gather.31.cloned.1.call-update) | async-done | bytes 1048592 | tf_op jit(solution)/shard_map/all_gather | solution.py:28
  183.6 18.8 %all_gather.60 = bf16[192,1024]{1,0:T(8,128)(2,1)} all-gather(bf16[192,256]{1,0:T(8,128)(2,1)S(1)} %copy-done.36), channel_id=1, replica_groups=mesh['groups'=2,'tm'=4,'chan'=4] {'chan'}, dimensions={1}, use_global_device_ids=true | all-gather | bytes 491520 | tf_op jit(solution)/shard_map/all_gather | solution.py:60
  202.4 6.5 %all-gather.11 = bf16[1,256,1024]{2,1,0:T(8,128)(2,1)S(1)} all-gather(bf16[1,256,256]{2,1,0:T(8,128)(2,1)S(1)} %copy-done.33), channel_id=13, replica_groups=mesh['groups'=2,'tm'=4,'chan'=4] {'tm'}, dimensions={2}, use_global_device_ids=true | all-gather | bytes 655360 | tf_op jit(solution)/shard_map/all_gather | solution.py:29
  216.7 5.0 %all-gather.33.cloned.1.call-done = bf16[1,2,1024,256]{3,2,1,0:T(8,128)(2,1)} async-done(((bf16[1,2,256,256]{3,2,1,0:T(8,128)(2,1)}), bf16[1,2,1024,256]{3,2,1,0:T(8,128)(2,1)}) %all-gather.33.cloned.1.call-update) | async-done | bytes 1048592 | tf_op jit(solution)/shard_map/all_gather | solution.py:27
  225.2 14.8 %all-gather.35.cloned.1.call-done = bf16[1,2,1024,256]{3,2,1,0:T(8,128)(2,1)} async-done(((bf16[1,2,256,256]{3,2,1,0:T(8,128)(2,1)}), bf16[1,2,1024,256]{3,2,1,0:T(8,128)(2,1)}) %all-gather.35.cloned.1.call-update) | async-done | bytes 1048592 | tf_op jit(solution)/shard_map/all_gather | solution.py:28
  246.1 20.9 %reduce-scatter.17.cloned.1.call-done = bf16[192,256]{1,0:T(8,128)(2,1)} async-done(((bf16[192,1024]{1,0:T(8,128)(2,1)}), bf16[192,256]{1,0:T(8,128)(2,1)}) %reduce-scatter.17.cloned.1.call-update) | async-done | bytes 98320 | tf_op jit(solution)/shard_map/reduce_scatter | solution.py:76
  268.7 14.3 %all_gather.61 = bf16[192,1024]{1,0:T(8,128)(2,1)S(1)} all-gather(bf16[192,256]{1,0:T(8,128)(2,1)S(1)} %add_convert_fusion.5), channel_id=1, replica_groups=mesh['groups'=2,'tm'=4,'chan'=4] {'chan'}, dimensions={1}, use_global_device_ids=true | all-gather | bytes 491520 | tf_op jit(solution)/shard_map/all_gather | solution.py:60
  286.3 19.8 %reduce-scatter.19.cloned.1.call-done = bf16[192,256]{1,0:T(8,128)(2,1)} async-done(((bf16[192,1024]{1,0:T(8,128)(2,1)}), bf16[192,256]{1,0:T(8,128)(2,1)}) %reduce-scatter.19.cloned.1.call-update) | async-done | bytes 98320 | tf_op jit(solution)/shard_map/reduce_scatter | solution.py:76
  307.7 14.6 %all_gather.62 = bf16[192,1024]{1,0:T(8,128)(2,1)S(1)} all-gather(bf16[192,256]{1,0:T(8,128)(2,1)S(1)} %add_convert_fusion.4), channel_id=1, replica_groups=mesh['groups'=2,'tm'=4,'chan'=4] {'chan'}, dimensions={1}, use_global_device_ids=true | all-gather | bytes 491520 | tf_op jit(solution)/shard_map/all_gather | solution.py:60
  325.8 8.0 %collective-permute-done.14 = bf16[192,1024]{1,0:T(8,128)(2,1)S(1)} collective-permute-done((bf16[192,1024]{1,0:T(8,128)(2,1)S(1)}, bf16[192,1024]{1,0:T(8,128)(2,1)S(1)}, u32[]{:S(2)}, u32[]{:S(2)}) %collective-permute-start.14) | collective-permute-done | bytes 393248 | tf_op jit(solution)/shard_map/ppermute | solution.py:10
  336.9 16.6 %reduce-scatter.21.cloned.1.call-done = bf16[192,256]{1,0:T(8,128)(2,1)} async-done(((bf16[192,1024]{1,0:T(8,128)(2,1)}), bf16[192,256]{1,0:T(8,128)(2,1)}) %reduce-scatter.21.cloned.1.call-update) | async-done | bytes 98320 | tf_op jit(solution)/shard_map/reduce_scatter | solution.py:76
  354.5 15.8 %all_gather.63 = bf16[192,1024]{1,0:T(8,128)(2,1)S(1)} all-gather(bf16[192,256]{1,0:T(8,128)(2,1)S(1)} %add_convert_fusion.3), channel_id=1, replica_groups=mesh['groups'=2,'tm'=4,'chan'=4] {'chan'}, dimensions={1}, use_global_device_ids=true | all-gather | bytes 491520 | tf_op jit(solution)/shard_map/all_gather | solution.py:60
  379.4 20.9 %reduce-scatter.23.cloned.1.call-done = bf16[192,256]{1,0:T(8,128)(2,1)} async-done(((bf16[192,1024]{1,0:T(8,128)(2,1)}), bf16[192,256]{1,0:T(8,128)(2,1)}) %reduce-scatter.23.cloned.1.call-update) | async-done | bytes 98320 | tf_op jit(solution)/shard_map/reduce_scatter | solution.py:76
  (197 shorter events, 90.8 us)
Async XLA Ops:
  7.2 28.6 %all-gather.21.cloned.1.call-start = ((), (), s32[]{:S(2)}) async-start(), calls=%async_computation.16 | async-start | bytes 1310720 | tf_op jit(solution)/shard_map/all_gather | solution.py:27
  9.5 37.9 %all-gather.23.cloned.1.call-start = ((), (), s32[]{:S(2)}) async-start(), calls=%async_computation.17 | async-start | bytes 1310720 | tf_op jit(solution)/shard_map/all_gather | solution.py:28
  10.6 64.8 %reduce-scatter.9.cloned.1.call-start = ((), (), s32[]{:S(2)}) async-start(), calls=%async_computation.8 | async-start | bytes 491520 | tf_op jit(solution)/shard_map/reduce_scatter | solution.py:51
  11.5 7.9 %collective-permute-start = (bf16[192,256]{1,0:T(8,128)(2,1)S(1)}, bf16[192,256]{1,0:T(8,128)(2,1)S(1)}, u32[]{:S(2)}, u32[]{:S(2)}) collective-permute-start(bf16[192,256]{1,0:T(8,128)(2,1)S(1)} %copy-done.35), channel_id=1, source_target_pairs={{0,1},{1,2},{2,3},{3,0},{4,5},{5,6},{6,7},{7,4},{8,9},{9,10},{10,1... | collective-permute-start | bytes 294920 | tf_op jit(solution)/shard_map/ppermute | solution.py:33
  25.8 7.2 %collective-permute-start.2 = (bf16[192,256]{1,0:T(8,128)(2,1)S(1)}, bf16[192,256]{1,0:T(8,128)(2,1)S(1)}, u32[]{:S(2)}, u32[]{:S(2)}) collective-permute-start(bf16[192,256]{1,0:T(8,128)(2,1)S(1)} %collective-permute-done.1), channel_id=1, source_target_pairs={{0,1},{1,2},{2,3},{3,0},{4,5},{5,6},{6,7},{7,4},{8,9},{9,10},{10,1... | collective-permute-start | bytes 294920 | tf_op jit(solution)/shard_map/ppermute | solution.py:33
  33.5 15.3 %collective-permute-start.3 = (bf16[192,1024]{1,0:T(8,128)(2,1)S(1)}, bf16[192,1024]{1,0:T(8,128)(2,1)S(1)}, u32[]{:S(2)}, u32[]{:S(2)}) collective-permute-start(bf16[192,1024]{1,0:T(8,128)(2,1)S(1)} %fusion.74), channel_id=1, source_target_pairs={{0,4},{4,8},{8,12},{1,5},{5,9},{9,13},{2,6},{6,10},{10,14},{3,7},{... | collective-permute-start | bytes 1179656 | tf_op jit(solution)/shard_map/ppermute | solution.py:10
  51.5 49.1 %all-gather.25.cloned.1.call-start = ((), (), s32[]{:S(2)}) async-start(), calls=%async_computation.18 | async-start | bytes 1310720 | tf_op jit(solution)/shard_map/all_gather | solution.py:27
  52.1 60.0 %all-gather.27.cloned.1.call-start = ((), (), s32[]{:S(2)}) async-start(), calls=%async_computation.19 | async-start | bytes 1310720 | tf_op jit(solution)/shard_map/all_gather | solution.py:28
  52.7 89.9 %reduce-scatter.11.cloned.1.call-start = ((), (), s32[]{:S(2)}) async-start(), calls=%async_computation.9 | async-start | bytes 491520 | tf_op jit(solution)/shard_map/reduce_scatter | solution.py:51
  97.2 17.2 %collective-permute-start.7 = (bf16[192,1024]{1,0:T(8,128)(2,1)S(1)}, bf16[192,1024]{1,0:T(8,128)(2,1)}, u32[]{:S(2)}, u32[]{:S(2)}) collective-permute-start(bf16[192,1024]{1,0:T(8,128)(2,1)S(1)} %fusion.67), channel_id=1, source_target_pairs={{0,8},{4,12},{1,9},{5,13},{2,10},{6,14},{3,11},{7,15},{16,24},{20,... | collective-permute-start | bytes 1179656 | tf_op jit(solution)/shard_map/ppermute | solution.py:10
  118.8 40.2 %all-gather.29.cloned.1.call-start = ((), (), s32[]{:S(2)}) async-start(), calls=%async_computation.20 | async-start | bytes 1310720 | tf_op jit(solution)/shard_map/all_gather | solution.py:27
  119.6 57.8 %all-gather.31.cloned.1.call-start = ((), (), s32[]{:S(2)}) async-start(), calls=%async_computation.21 | async-start | bytes 1310720 | tf_op jit(solution)/shard_map/all_gather | solution.py:28
  120.3 88.5 %reduce-scatter.13.cloned.1.call-start = ((), (), s32[]{:S(2)}) async-start(), calls=%async_computation.10 | async-start | bytes 491520 | tf_op jit(solution)/shard_map/reduce_scatter | solution.py:51
  150.6 9.8 %collective-permute-start.9 = (bf16[192,256]{1,0:T(8,128)(2,1)S(1)}, bf16[192,256]{1,0:T(8,128)(2,1)S(1)}, u32[]{:S(2)}, u32[]{:S(2)}) collective-permute-start(bf16[192,256]{1,0:T(8,128)(2,1)S(1)} %collective-permute-done.8), channel_id=1, source_target_pairs={{0,1},{1,2},{2,3},{3,0},{4,5},{5,6},{6,7},{7,4},{8,9},{9,10},{10,1... | collective-permute-start | bytes 294920 | tf_op jit(solution)/shard_map/ppermute | solution.py:33
  160.4 18.4 %collective-permute-start.10 = (bf16[192,256]{1,0:T(8,128)(2,1)S(1)}, bf16[192,256]{1,0:T(8,128)(2,1)S(1)}, u32[]{:S(2)}, u32[]{:S(2)}) collective-permute-start(bf16[192,256]{1,0:T(8,128)(2,1)S(1)} %collective-permute-done.9), channel_id=1, source_target_pairs={{0,1},{1,2},{2,3},{3,0},{4,5},{5,6},{6,7},{7,4},{8,9},{9,10},{10,1... | collective-permute-start | bytes 294920 | tf_op jit(solution)/shard_map/ppermute | solution.py:33
  182.0 39.7 %all-gather.33.cloned.1.call-start = ((), (), s32[]{:S(2)}) async-start(), calls=%async_computation.22 | async-start | bytes 1310720 | tf_op jit(solution)/shard_map/all_gather | solution.py:27
  182.6 57.4 %all-gather.35.cloned.1.call-start = ((), (), s32[]{:S(2)}) async-start(), calls=%async_computation.23 | async-start | bytes 1310720 | tf_op jit(solution)/shard_map/all_gather | solution.py:28
  183.3 83.6 %reduce-scatter.17.cloned.1.call-start = ((), (), s32[]{:S(2)}) async-start(), calls=%async_computation.12 | async-start | bytes 491520 | tf_op jit(solution)/shard_map/reduce_scatter | solution.py:76
  223.7 17.7 %collective-permute-start.13 = (bf16[192,256]{1,0:T(8,128)(2,1)}, bf16[192,256]{1,0:T(8,128)(2,1)}, u32[]{:S(2)}, u32[]{:S(2)}) collective-permute-start(bf16[192,256]{1,0:T(8,128)(2,1)} %collective-permute-done.12), channel_id=1, source_target_pairs={{0,1},{1,2},{2,3},{3,0},{4,5},{5,6},{6,7},{7,4},{8,9},{9,10},{10,1... | collective-permute-start | bytes 294920 | tf_op jit(solution)/shard_map/ppermute | solution.py:33
  246.0 60.0 %reduce-scatter.19.cloned.1.call-start = ((), (), s32[]{:S(2)}) async-start(), calls=%async_computation.13 | async-start | bytes 491520 | tf_op jit(solution)/shard_map/reduce_scatter | solution.py:76
  286.2 67.4 %reduce-scatter.21.cloned.1.call-start = ((), (), s32[]{:S(2)}) async-start(), calls=%async_computation.14 | async-start | bytes 491520 | tf_op jit(solution)/shard_map/reduce_scatter | solution.py:76
  324.1 9.7 %collective-permute-start.14 = (bf16[192,1024]{1,0:T(8,128)(2,1)S(1)}, bf16[192,1024]{1,0:T(8,128)(2,1)S(1)}, u32[]{:S(2)}, u32[]{:S(2)}) collective-permute-start(bf16[192,1024]{1,0:T(8,128)(2,1)S(1)} %fusion.2), channel_id=1, source_target_pairs={{8,0},{12,4},{9,1},{13,5},{10,2},{14,6},{11,3},{15,7},{24,16},{28,... | collective-permute-start | bytes 1179656 | tf_op jit(solution)/shard_map/ppermute | solution.py:10
  334.9 42.0 %reduce-scatter.15.cloned.1.call-start = ((), (), s32[]{:S(2)}) async-start(), calls=%async_computation.11 | async-start | bytes 491520 | tf_op jit(solution)/shard_map/reduce_scatter | solution.py:51
  336.9 63.3 %reduce-scatter.23.cloned.1.call-start = ((), (), s32[]{:S(2)}) async-start(), calls=%async_computation.15 | async-start | bytes 491520 | tf_op jit(solution)/shard_map/reduce_scatter | solution.py:76
  (49 other events, 370.6 us)
Sparse Core Ops, SparseCore 0:
  9.6 19.4 all-gather.20
  30.7 16.6 all-gather.22
  51.7 23.7 reduce-scatter.8
  76.8 14.9 all-gather.24
  93.2 18.8 all-gather.26
  118.9 23.6 reduce-scatter.10
  144.2 14.8 all-gather.28
  160.6 16.6 all-gather.30
  182.1 22.2 reduce-scatter.12
  205.9 15.7 all-gather.32
  223.3 16.6 all-gather.34
  246.1 20.7 reduce-scatter.16
  286.3 19.6 reduce-scatter.18
  335.1 18.4 reduce-scatter.20
  355.7 19.9 reduce-scatter.14
  377.8 22.3 reduce-scatter.22
